TPU v7x, 32 devices: a whole 2x2x4 slice. The times are simulated.
32 devices in a mesh: view: 4 (over x, core), samp: 8 (over z, y).
Axes of the slice: x: 2, y: 2, z: 4, core: 2. Of those that a mesh axis runs over, the one named last changes fastest.
Arguments:
- view_data: bfloat16 [8, 4096, 2048], P('view', 'samp'), may hold values from -10 to 10
- init_coeffs: float32 [8, 2048, 128], P('view'), may hold values from -0.125 to 0.125
Outputs:
- shared_scores: float32 [4096, 128], P('samp')
- final_coeffs: float32 [8, 2048, 128], P('view', 'samp')
All inputs are finite; a program needn't handle non-finite values.
Results may differ from a plain program's by a relative error of at most 0.005.
Values may be sent and summed in bfloat16 or wider, within the bound.
No kernel may reach another device: no remote copies, remote signals or barrier semaphores. Data moves between devices by JAX's collectives and lax.ppermute only.
A program may use at most 128 MiB of HBM per device.

v0:
```python
import jax
import jax.numpy as jnp
from jax import lax
from jax.sharding import PartitionSpec as P

OUTER = 2
INNER = 2
NS_ITERS = 12
HIGH = lax.Precision.HIGHEST
ridge_weight = 0.1
step_size = 0.5


def newton_inverse(gram):
    size_k = gram.shape[0]
    eye_mat = jnp.eye(size_k, dtype=jnp.float32)
    shrunk = gram + jnp.trace(gram) / size_k * eye_mat
    scale = jnp.sqrt(jnp.sum(shrunk * shrunk))
    approx = shrunk / scale
    inverse = eye_mat
    for turn in range(NS_ITERS):
        factor = 0.5 * (3.0 * eye_mat - jnp.dot(inverse, approx, precision=HIGH))
        approx = jnp.dot(approx, factor, precision=HIGH)
        inverse = jnp.dot(factor, inverse, precision=HIGH)
    return (inverse, scale)


def make_scores(view_data, coeffs_low, total):
    local_sum = jnp.zeros((view_data.shape[1], coeffs_low.shape[2]), jnp.float32)
    for member in range(view_data.shape[0]):
        local_sum = local_sum + jnp.dot(
            view_data[member], coeffs_low[member], preferred_element_type=jnp.float32
        )
    summed = lax.psum(local_sum, "view")
    gram = lax.psum(jnp.dot(summed.T, summed, precision=HIGH), "samp")
    inverse, scale = newton_inverse(gram)
    return jnp.dot(summed, inverse, precision=HIGH) * jnp.sqrt(total / scale)


def grad_term(samples, weights_low, scores):
    resid = (jnp.dot(samples, weights_low, preferred_element_type=jnp.float32) - scores).astype(
        jnp.bfloat16
    )
    return lax.dot_general(
        samples, resid, (((0,), (0,)), ((), ())), preferred_element_type=jnp.float32
    )


def body(view_data, init_coeffs):
    total = view_data.shape[1] * lax.axis_size("samp")
    row_count = init_coeffs.shape[1] // lax.axis_size("samp")
    row_start = lax.axis_index("samp") * row_count
    own_coeffs = lax.dynamic_slice_in_dim(init_coeffs, row_start, row_count, 1)
    coeffs_low = init_coeffs.astype(jnp.bfloat16)
    scores = make_scores(view_data, coeffs_low, total)
    for outer_step in range(OUTER):
        for inner_step in range(INNER):
            terms = jnp.stack(
                [
                    grad_term(view_data[member], coeffs_low[member], scores)
                    for member in range(view_data.shape[0])
                ]
            )
            summed_grad = lax.psum_scatter(terms, "samp", scatter_dimension=1, tiled=True)
            own_coeffs = own_coeffs - step_size * (summed_grad / total + ridge_weight * own_coeffs)
            coeffs_low = lax.all_gather(own_coeffs.astype(jnp.bfloat16), "samp", axis=1, tiled=True)
        scores = make_scores(view_data, coeffs_low, total)
    return (scores, own_coeffs)


def solution(mesh):
    in_specs = (P("view", "samp", None), P("view", None, None))
    out_specs = (P("samp", None), P("view", "samp", None))
    return jax.shard_map(body, mesh=mesh, in_specs=in_specs, out_specs=out_specs, check_vma=False)
```

profile of v0, /device:TPU:0, one launch (start us, length us, event | category | flops | bytes accessed | tf_op | source)
XLA Modules:
  0.0 856.1 jit_solution(11644975215844309981)
XLA Ops:
  7.2 1.9 convert_element_type.42
  9.1 2.3 fusion.12
  11.4 1.4 fusion.163
  12.9 35.1 %all-reduce.7.cloned.1.call-done = f32[512,128]{1,0:T(8,128)} async-done(((f32[512,128]{1,0:T(8,128)}), f32[512,128]{1,0:T(8,128)}) %all-reduce.7.cloned.1.call-update) | async-done | bytes 262160 | tf_op jit(solution)/shard_map/psum | solution.py:34
  48.0 2.2 fusion.165
  50.4 70.9 %all-reduce.9.cloned.1.call-done = f32[128,128]{1,0:T(8,128)} async-done(((f32[128,128]{1,0:T(8,128)}), f32[128,128]{1,0:T(8,128)}) %all-reduce.9.cloned.1.call-update) | async-done | bytes 65552 | tf_op jit(solution)/shard_map/psum | solution.py:35
  121.3 1.5 select_reduce_fusion.2
  123.4 1.5 multiply_reduce_fusion.2
  125.6 1.0 fusion.119
  126.8 1.1 fusion.152
  127.9 0.2 fusion.118
  129.8 0.2 fusion.115
  134.8 0.4 convolution_multiply_fusion.2
  135.1 2.3 convolution_bitcast_fusion.6
  137.6 0.5 convolution_bitcast_fusion.7
  138.0 1.5 pad_maximum_fusion
  139.6 1.0 constant_dynamic-slice_fusion
  140.7 67.8 %reduce-scatter.5.cloned.1.call-done = f32[2,256,128]{1,2,0:T(8,128)} async-done(((f32[2,2048,128]{1,2,0:T(8,128)}), f32[2,256,128]{1,2,0:T(8,128)}) %reduce-scatter.5.cloned.1.call-update) | async-done | bytes 262160 | tf_op jit(solution)/shard_map/reduce_scatter | solution.py:64
  208.5 1.7 fusion.144
  210.3 39.2 %all-gather.5.cloned.1.call-done = bf16[2,2048,128]{1,2,0:T(8,128)(2,1)} async-done(((bf16[2,256,128]{1,2,0:T(8,128)(2,1)}), bf16[2,2048,128]{1,2,0:T(8,128)(2,1)}) %all-gather.5.cloned.1.call-update) | async-done | bytes 1048592 | tf_op jit(solution)/shard_map/all_gather | solution.py:66
  249.5 4.0 convolution_bitcast_fusion.4
  253.4 4.0 convolution_bitcast_fusion.5
  257.4 1.5 pad_maximum_fusion.1
  259.0 68.0 %reduce-scatter.7.cloned.1.call-done = f32[2,256,128]{1,2,0:T(8,128)} async-done(((f32[2,2048,128]{1,2,0:T(8,128)}), f32[2,256,128]{1,2,0:T(8,128)}) %reduce-scatter.7.cloned.1.call-update) | async-done | bytes 262160 | tf_op jit(solution)/shard_map/reduce_scatter | solution.py:64
  327.0 1.7 fusion.162
  328.7 39.1 %all-gather.7.cloned.1.call-done = bf16[2,2048,128]{1,2,0:T(8,128)(2,1)} async-done(((bf16[2,256,128]{1,2,0:T(8,128)(2,1)}), bf16[2,2048,128]{1,2,0:T(8,128)(2,1)}) %all-gather.7.cloned.1.call-update) | async-done | bytes 1048592 | tf_op jit(solution)/shard_map/all_gather | solution.py:66
  367.9 2.7 fusion.55
  370.6 3.1 fusion.164
  373.7 0.2 all-reduce.13.cloned.1.call-start
  374.0 31.2 %all-reduce.11.cloned.1.call-done = f32[512,128]{0,1:T(8,128)} async-done(((f32[512,128]{0,1:T(8,128)}), f32[512,128]{0,1:T(8,128)}) %all-reduce.11.cloned.1.call-update) | async-done | bytes 262160 | tf_op jit(solution)/shard_map/psum | solution.py:34
  405.2 2.0 fusion.187
  407.3 71.1 %all-reduce.13.cloned.1.call-done = f32[128,128]{1,0:T(8,128)} async-done(((f32[128,128]{1,0:T(8,128)}), f32[128,128]{1,0:T(8,128)}) %all-reduce.13.cloned.1.call-update) | async-done | bytes 65552 | tf_op jit(solution)/shard_map/psum | solution.py:35
  478.4 1.5 select_reduce_fusion.1
  480.6 1.5 multiply_reduce_fusion.1
  482.8 1.0 fusion.107
  484.0 1.1 fusion.149
  485.0 0.2 fusion.106
  487.6 0.2 fusion.102
  490.8 0.2 fusion.97
  491.9 0.4 convolution_multiply_fusion.1
  492.3 2.3 convolution_bitcast_fusion.2
  494.7 0.4 convolution_bitcast_fusion.3
  495.2 1.5 pad_maximum_fusion.2
  496.7 69.1 %reduce-scatter.9.cloned.1.call-done = f32[2,256,128]{1,2,0:T(8,128)} async-done(((f32[2,2048,128]{1,2,0:T(8,128)}), f32[2,256,128]{1,2,0:T(8,128)}) %reduce-scatter.9.cloned.1.call-update) | async-done | bytes 262160 | tf_op jit(solution)/shard_map/reduce_scatter | solution.py:64
  565.8 1.7 fusion.145
  567.5 39.2 %all-gather.9.cloned.1.call-done = bf16[2,2048,128]{1,2,0:T(8,128)(2,1)} async-done(((bf16[2,256,128]{1,2,0:T(8,128)(2,1)}), bf16[2,2048,128]{1,2,0:T(8,128)(2,1)}) %all-gather.9.cloned.1.call-update) | async-done | bytes 1048592 | tf_op jit(solution)/shard_map/all_gather | solution.py:66
  606.7 3.6 convolution_bitcast_fusion
  610.3 3.6 convolution_bitcast_fusion.1
  613.9 1.5 pad_maximum_fusion.3
  615.5 68.0 %reduce-scatter.11.cloned.1.call-done = f32[2,256,128]{1,2,0:T(8,128)} async-done(((f32[2,2048,128]{1,2,0:T(8,128)}), f32[2,256,128]{1,2,0:T(8,128)}) %reduce-scatter.11.cloned.1.call-update) | async-done | bytes 262160 | tf_op jit(solution)/shard_map/reduce_scatter | solution.py:64
  683.5 1.7 fusion.161
  685.3 39.1 %all-gather.11.cloned.1.call-done = bf16[2,2048,128]{1,2,0:T(8,128)(2,1)} async-done(((bf16[2,256,128]{1,2,0:T(8,128)(2,1)}), bf16[2,2048,128]{1,2,0:T(8,128)(2,1)}) %all-gather.11.cloned.1.call-update) | async-done | bytes 1048592 | tf_op jit(solution)/shard_map/all_gather | solution.py:66
  724.4 2.7 fusion
  727.1 3.1 fusion.46
  730.3 0.3 all-reduce.17.cloned.1.call-start
  730.5 31.2 %all-reduce.15.cloned.1.call-done = f32[512,128]{0,1:T(8,128)} async-done(((f32[512,128]{0,1:T(8,128)}), f32[512,128]{0,1:T(8,128)}) %all-reduce.15.cloned.1.call-update) | async-done | bytes 262160 | tf_op jit(solution)/shard_map/psum | solution.py:34
  761.7 2.0 fusion.209
  763.8 0.8 copy.6
  764.6 70.2 %all-reduce.17.cloned.1.call-done = f32[128,128]{1,0:T(8,128)} async-done(((f32[128,128]{1,0:T(8,128)}), f32[128,128]{1,0:T(8,128)}) %all-reduce.17.cloned.1.call-update) | async-done | bytes 65552 | tf_op jit(solution)/shard_map/psum | solution.py:35
  834.8 1.5 select_reduce_fusion
  837.0 1.5 multiply_reduce_fusion
  839.2 1.0 fusion.95
  840.4 1.1 fusion.146
  848.3 1.3 convolution_multiply_fusion
  (141 shorter events, 20.3 us)
Async XLA Ops:
  7.2 40.9 %all-reduce.7.cloned.1.call-start = ((), (), s32[]{:S(2)}) async-start(), calls=%async_computation.4 | async-start | bytes 524288 | tf_op jit(solution)/shard_map/psum | solution.py:34
  7.2 4.2 copy-start
  12.9 108.4 %all-reduce.9.cloned.1.call-start = ((), (), s32[]{:S(2)}) async-start(), calls=%async_computation.5 | async-start | bytes 131072 | tf_op jit(solution)/shard_map/psum | solution.py:35
  50.3 158.2 %reduce-scatter.5.cloned.1.call-start = ((), (), s32[]{:S(2)}) async-start(), calls=%async_computation.6 | async-start | bytes 2359296 | tf_op jit(solution)/shard_map/reduce_scatter | solution.py:64
  130.2 4.5 copy-start.4
  134.7 2.8 copy-start.1
  139.6 109.9 %all-gather.5.cloned.1.call-start = ((), (), s32[]{:S(2)}) async-start(), calls=%async_computation.7 | async-start | bytes 1179648 | tf_op jit(solution)/shard_map/all_gather | solution.py:66
  210.2 116.8 %reduce-scatter.7.cloned.1.call-start = ((), (), s32[]{:S(2)}) async-start(), calls=%async_computation.8 | async-start | bytes 2359296 | tf_op jit(solution)/shard_map/reduce_scatter | solution.py:64
  258.9 68.1 %copy-start.6 = (f32[2,256,128]{1,2,0:T(8,128)S(1)}, f32[2,256,128]{1,2,0:T(8,128)}, u32[]{:S(2)}) copy-start(f32[2,256,128]{1,2,0:T(8,128)} %reduce-scatter.5.cloned.1.call-done) | copy-start | bytes 786436
  258.9 109.0 %all-gather.7.cloned.1.call-start = ((), (), s32[]{:S(2)}) async-start(), calls=%async_computation.9 | async-start | bytes 1179648 | tf_op jit(solution)/shard_map/all_gather | solution.py:66
  328.7 76.5 %all-reduce.11.cloned.1.call-start = ((), (), s32[]{:S(2)}) async-start(), calls=%async_computation.10 | async-start | bytes 524288 | tf_op jit(solution)/shard_map/psum | solution.py:34
  367.9 2.7 copy-start.8
  373.7 104.7 %all-reduce.13.cloned.1.call-start = ((), (), s32[]{:S(2)}) async-start(), calls=%async_computation.11 | async-start | bytes 131072 | tf_op jit(solution)/shard_map/psum | solution.py:35
  407.3 158.5 %reduce-scatter.9.cloned.1.call-start = ((), (), s32[]{:S(2)}) async-start(), calls=%async_computation.12 | async-start | bytes 2359296 | tf_op jit(solution)/shard_map/reduce_scatter | solution.py:64
  487.4 4.5 copy-start.5
  491.9 2.8 copy-start.2
  496.7 110.0 %all-gather.9.cloned.1.call-start = ((), (), s32[]{:S(2)}) async-start(), calls=%async_computation.13 | async-start | bytes 1179648 | tf_op jit(solution)/shard_map/all_gather | solution.py:66
  567.5 116.0 %reduce-scatter.11.cloned.1.call-start = ((), (), s32[]{:S(2)}) async-start(), calls=%async_computation.14 | async-start | bytes 2359296 | tf_op jit(solution)/shard_map/reduce_scatter | solution.py:64
  615.4 68.1 %copy-start.7 = (f32[2,256,128]{1,2,0:T(8,128)S(1)}, f32[2,256,128]{1,2,0:T(8,128)}, u32[]{:S(2)}) copy-start(f32[2,256,128]{1,2,0:T(8,128)} %reduce-scatter.9.cloned.1.call-done) | copy-start | bytes 786436
  615.4 109.0 %all-gather.11.cloned.1.call-start = ((), (), s32[]{:S(2)}) async-start(), calls=%async_computation.15 | async-start | bytes 1179648 | tf_op jit(solution)/shard_map/all_gather | solution.py:66
  685.2 76.5 %all-reduce.15.cloned.1.call-start = ((), (), s32[]{:S(2)}) async-start(), calls=%async_computation.16 | async-start | bytes 524288 | tf_op jit(solution)/shard_map/psum | solution.py:34
  724.4 2.7 copy-start.9
  730.3 104.6 %all-reduce.17.cloned.1.call-start = ((), (), s32[]{:S(2)}) async-start(), calls=%async_computation.17 | async-start | bytes 131072 | tf_op jit(solution)/shard_map/psum | solution.py:35
  843.8 4.5 copy-start.3
Sparse Core Ops, SparseCore 0:
  13.0 35.0 all-reduce.6
  52.0 69.2 all-reduce.8
  139.7 68.8 reduce-scatter.4
  211.0 38.3 all-gather.4
  259.0 67.8 reduce-scatter.6
  329.4 38.4 all-gather.6
  373.9 31.2 all-reduce.10
  409.2 69.2 all-reduce.12
  496.8 68.9 reduce-scatter.8
  568.2 38.3 all-gather.8
  615.6 67.9 reduce-scatter.10
  686.0 38.3 all-gather.10
  730.4 31.2 all-reduce.14
  765.6 69.2 all-reduce.16
where the time goes:
time: 857 us; the launch traced here: 856 us
  waiting for transfers between devices  740 us (86%)
  matrix products  70.7 us (8%)
  other arithmetic  23.3 us (3%)
  between operations  19.3 us (2%)
    reduce_scatter x4, waiting for transfers between devices, body(): lax.psum_scatter(terms, 'samp', scatter_dimension=1, tiled=True)  273 us
    psum x3, waiting for transfers between devices, make_scores(): gram = lax.psum(jnp.dot(summed.T, summed, precision=HIGH), 'samp')  212 us
    all_gather x4, waiting for transfers between devices, body(): lax.all_gather(own_coeffs.astype(jnp.bfloat16), 'samp', axis=1, tiled=True)  157 us
    psum x3, waiting for transfers between devices, make_scores(): summed = lax.psum(local_sum, 'view')  97.5 us
    dot_general x8, matrix products, grad_term(): lax.dot_general(samples, resid, (((0,), (0,)), ((), ())), preferred_eleme...  20.6 us
  transfers between devices with their start and end apart: 14, of which 14 were waited for; matrix products, arithmetic and copies ran while one was open for 0% of the time, Pallas kernels for 0%

commit v1 on v0

--- a/solution.py
+++ b/solution.py
@@ -31,7 +31,7 @@
         local_sum = local_sum + jnp.dot(
             view_data[member], coeffs_low[member], preferred_element_type=jnp.float32
         )
-    summed = lax.psum(local_sum, "view")
+    summed = jnp.sum(jax.lax.all_gather(local_sum, "view"), axis=0)
     gram = lax.psum(jnp.dot(summed.T, summed, precision=HIGH), "samp")
     inverse, scale = newton_inverse(gram)
     return jnp.dot(summed, inverse, precision=HIGH) * jnp.sqrt(total / scale)

time: 857 us -> 811 us (0.946)
  waiting for transfers between devices: 740 us -> 690 us
    psum x3 -> x0, waiting for transfers between devices: 97.5 us -> none  [make_scores(): summed = lax.psum(local_sum, 'view')]
    all_gather x0 -> x3, waiting for transfers between devices: none -> 50.8 us  [make_scores(): summed = jnp.sum(jax.lax.all_gather(local_sum, 'view'), axis=0)]
where the time goes in v1:
time: 811 us; the launch traced here: 810 us
  waiting for transfers between devices  690 us (85%)
  matrix products  67.5 us (8%)
  other arithmetic  25.9 us (3%)
  between operations  19.2 us (2%)
    reduce_scatter x4, waiting for transfers between devices, body(): lax.psum_scatter(terms, 'samp', scatter_dimension=1, tiled=True)  273 us
    psum x3, waiting for transfers between devices, make_scores(): gram = lax.psum(jnp.dot(summed.T, summed, precision=HIGH), 'samp')  209 us
    all_gather x4, waiting for transfers between devices, body(): lax.all_gather(own_coeffs.astype(jnp.bfloat16), 'samp', axis=1, tiled=True)  157 us
    all_gather x3, waiting for transfers between devices, make_scores(): summed = jnp.sum(jax.lax.all_gather(local_sum, 'view'), axis=0)  50.8 us
    dot_general x8, matrix products, grad_term(): lax.dot_general(samples, resid, (((0,), (0,)), ((), ())), preferred_eleme...  20.6 us
  transfers between devices with their start and end apart: 14, of which 14 were waited for; matrix products, arithmetic and copies ran while one was open for 0% of the time, Pallas kernels for 0%

profile of v1, /device:TPU:0, one launch (start us, length us, event | category | flops | bytes accessed | tf_op | source)
XLA Modules:
  0.0 809.9 jit_solution(13586449834848094274)
XLA Ops:
  7.2 1.9 convert_element_type.42
  9.1 2.3 fusion.12
  11.4 1.4 fusion.163
  12.9 19.5 %all-gather.19.cloned.1.call-done = f32[2048,128]{1,0:T(8,128)} async-done(((f32[512,128]{1,0:T(8,128)}), f32[2048,128]{1,0:T(8,128)}) %all-gather.19.cloned.1.call-update) | async-done | bytes 1048592 | tf_op jit(solution)/shard_map/all_gather | solution.py:34
  32.4 1.3 reduce_sum.76
  33.8 1.2 fusion.165
  35.1 70.7 %all-reduce.4.cloned.1.call-done = f32[128,128]{1,0:T(8,128)} async-done(((f32[128,128]{1,0:T(8,128)}), f32[128,128]{1,0:T(8,128)}) %all-reduce.4.cloned.1.call-update) | async-done | bytes 65552 | tf_op jit(solution)/shard_map/psum | solution.py:35
  105.7 1.5 select_reduce_fusion.2
  107.8 1.5 multiply_reduce_fusion.2
  110.0 1.0 fusion.119
  111.2 1.1 fusion.152
  119.2 0.4 convolution_multiply_fusion.2
  119.5 2.3 convolution_bitcast_fusion.6
  122.0 0.5 convolution_bitcast_fusion.7
  122.4 1.5 pad_maximum_fusion
  124.0 1.0 constant_dynamic-slice_fusion
  125.1 68.1 %reduce-scatter.5.cloned.1.call-done = f32[2,256,128]{1,2,0:T(8,128)} async-done(((f32[2,2048,128]{1,2,0:T(8,128)}), f32[2,256,128]{1,2,0:T(8,128)}) %reduce-scatter.5.cloned.1.call-update) | async-done | bytes 262160 | tf_op jit(solution)/shard_map/reduce_scatter | solution.py:64
  193.3 1.7 fusion.144
  195.0 39.2 %all-gather.11.cloned.1.call-done = bf16[2,2048,128]{1,2,0:T(8,128)(2,1)} async-done(((bf16[2,256,128]{1,2,0:T(8,128)(2,1)}), bf16[2,2048,128]{1,2,0:T(8,128)(2,1)}) %all-gather.11.cloned.1.call-update) | async-done | bytes 1048592 | tf_op jit(solution)/shard_map/all_gather | solution.py:66
  234.2 4.0 convolution_bitcast_fusion.4
  238.1 4.0 convolution_bitcast_fusion.5
  242.1 1.5 pad_maximum_fusion.1
  243.7 68.0 %reduce-scatter.7.cloned.1.call-done = f32[2,256,128]{1,2,0:T(8,128)} async-done(((f32[2,2048,128]{1,2,0:T(8,128)}), f32[2,256,128]{1,2,0:T(8,128)}) %reduce-scatter.7.cloned.1.call-update) | async-done | bytes 262160 | tf_op jit(solution)/shard_map/reduce_scatter | solution.py:64
  311.7 1.7 fusion.162
  313.4 39.1 %all-gather.13.cloned.1.call-done = bf16[2,2048,128]{1,2,0:T(8,128)(2,1)} async-done(((bf16[2,256,128]{1,2,0:T(8,128)(2,1)}), bf16[2,2048,128]{1,2,0:T(8,128)(2,1)}) %all-gather.13.cloned.1.call-update) | async-done | bytes 1048592 | tf_op jit(solution)/shard_map/all_gather | solution.py:66
  352.6 2.7 fusion.55
  355.3 3.1 fusion.164
  358.4 0.2 all-reduce.6.cloned.1.call-start
  358.7 15.6 %all-gather.21.cloned.1.call-done = f32[2048,128]{0,1:T(8,128)} async-done(((f32[512,128]{0,1:T(8,128)}), f32[2048,128]{0,1:T(8,128)}) %all-gather.21.cloned.1.call-update) | async-done | bytes 1048592 | tf_op jit(solution)/shard_map/all_gather | solution.py:34
  374.3 1.9 reshape.5
  376.2 0.6 reduce_sum.79
  376.9 1.0 fusion.187
  377.9 69.6 %all-reduce.6.cloned.1.call-done = f32[128,128]{1,0:T(8,128)} async-done(((f32[128,128]{1,0:T(8,128)}), f32[128,128]{1,0:T(8,128)}) %all-reduce.6.cloned.1.call-update) | async-done | bytes 65552 | tf_op jit(solution)/shard_map/psum | solution.py:35
  447.6 1.5 select_reduce_fusion.1
  449.7 1.5 multiply_reduce_fusion.1
  451.9 1.0 fusion.107
  453.1 1.1 fusion.149
  461.0 0.4 convolution_multiply_fusion.1
  461.4 2.2 convolution_bitcast_fusion.2
  463.8 0.4 convolution_bitcast_fusion.3
  464.3 1.5 pad_maximum_fusion.2
  465.8 68.9 %reduce-scatter.9.cloned.1.call-done = f32[2,256,128]{1,2,0:T(8,128)} async-done(((f32[2,2048,128]{1,2,0:T(8,128)}), f32[2,256,128]{1,2,0:T(8,128)}) %reduce-scatter.9.cloned.1.call-update) | async-done | bytes 262160 | tf_op jit(solution)/shard_map/reduce_scatter | solution.py:64
  534.8 1.7 fusion.145
  536.5 39.2 %all-gather.15.cloned.1.call-done = bf16[2,2048,128]{1,2,0:T(8,128)(2,1)} async-done(((bf16[2,256,128]{1,2,0:T(8,128)(2,1)}), bf16[2,2048,128]{1,2,0:T(8,128)(2,1)}) %all-gather.15.cloned.1.call-update) | async-done | bytes 1048592 | tf_op jit(solution)/shard_map/all_gather | solution.py:66
  575.7 3.6 convolution_bitcast_fusion
  579.3 3.6 convolution_bitcast_fusion.1
  582.9 1.5 pad_maximum_fusion.3
  584.5 68.4 %reduce-scatter.11.cloned.1.call-done = f32[2,256,128]{1,2,0:T(8,128)} async-done(((f32[2,2048,128]{1,2,0:T(8,128)}), f32[2,256,128]{1,2,0:T(8,128)}) %reduce-scatter.11.cloned.1.call-update) | async-done | bytes 262160 | tf_op jit(solution)/shard_map/reduce_scatter | solution.py:64
  652.9 1.7 fusion.161
  654.6 39.1 %all-gather.17.cloned.1.call-done = bf16[2,2048,128]{1,2,0:T(8,128)(2,1)} async-done(((bf16[2,256,128]{1,2,0:T(8,128)(2,1)}), bf16[2,2048,128]{1,2,0:T(8,128)(2,1)}) %all-gather.17.cloned.1.call-update) | async-done | bytes 1048592 | tf_op jit(solution)/shard_map/all_gather | solution.py:66
  693.8 2.7 fusion
  696.5 3.1 fusion.46
  699.6 0.3 all-reduce.8.cloned.1.call-start
  699.9 15.6 %all-gather.23.cloned.1.call-done = f32[2048,128]{0,1:T(8,128)} async-done(((f32[512,128]{0,1:T(8,128)}), f32[2048,128]{0,1:T(8,128)}) %all-gather.23.cloned.1.call-update) | async-done | bytes 1048592 | tf_op jit(solution)/shard_map/all_gather | solution.py:34
  715.5 1.9 reshape.6
  717.4 0.6 reduce_sum.82
  718.0 1.0 fusion.209
  719.1 0.8 copy.9
  719.9 68.7 %all-reduce.8.cloned.1.call-done = f32[128,128]{1,0:T(8,128)} async-done(((f32[128,128]{1,0:T(8,128)}), f32[128,128]{1,0:T(8,128)}) %all-reduce.8.cloned.1.call-update) | async-done | bytes 65552 | tf_op jit(solution)/shard_map/psum | solution.py:35
  788.6 1.5 select_reduce_fusion
  790.7 1.5 multiply_reduce_fusion
  792.9 1.0 fusion.95
  794.2 1.1 fusion.146
  802.0 1.3 convolution_multiply_fusion
  (140 shorter events, 21.3 us)
Async XLA Ops:
  7.2 25.3 %all-gather.19.cloned.1.call-start = ((), (), s32[]{:S(2)}) async-start(), calls=%async_computation.15 | async-start | bytes 1310720 | tf_op jit(solution)/shard_map/all_gather | solution.py:34
  7.2 4.2 copy-start
  12.9 92.9 %all-reduce.4.cloned.1.call-start = ((), (), s32[]{:S(2)}) async-start(), calls=%async_computation.4 | async-start | bytes 131072 | tf_op jit(solution)/shard_map/psum | solution.py:35
  35.0 158.3 %reduce-scatter.5.cloned.1.call-start = ((), (), s32[]{:S(2)}) async-start(), calls=%async_computation.5 | async-start | bytes 2359296 | tf_op jit(solution)/shard_map/reduce_scatter | solution.py:64
  119.1 2.8 copy-start.1
  124.0 110.2 %all-gather.11.cloned.1.call-start = ((), (), s32[]{:S(2)}) async-start(), calls=%async_computation.6 | async-start | bytes 1179648 | tf_op jit(solution)/shard_map/all_gather | solution.py:66
  194.9 116.7 %reduce-scatter.7.cloned.1.call-start = ((), (), s32[]{:S(2)}) async-start(), calls=%async_computation.7 | async-start | bytes 2359296 | tf_op jit(solution)/shard_map/reduce_scatter | solution.py:64
  243.6 68.1 %copy-start.3 = (f32[2,256,128]{1,2,0:T(8,128)S(1)}, f32[2,256,128]{1,2,0:T(8,128)}, u32[]{:S(2)}) copy-start(f32[2,256,128]{1,2,0:T(8,128)} %reduce-scatter.5.cloned.1.call-done) | copy-start | bytes 786436
  243.6 109.0 %all-gather.13.cloned.1.call-start = ((), (), s32[]{:S(2)}) async-start(), calls=%async_computation.8 | async-start | bytes 1179648 | tf_op jit(solution)/shard_map/all_gather | solution.py:66
  313.4 60.9 %all-gather.21.cloned.1.call-start = ((), (), s32[]{:S(2)}) async-start(), calls=%async_computation.16 | async-start | bytes 1310720 | tf_op jit(solution)/shard_map/all_gather | solution.py:34
  352.6 2.7 copy-start.5
  358.4 89.1 %all-reduce.6.cloned.1.call-start = ((), (), s32[]{:S(2)}) async-start(), calls=%async_computation.9 | async-start | bytes 131072 | tf_op jit(solution)/shard_map/psum | solution.py:35
  377.9 156.9 %reduce-scatter.9.cloned.1.call-start = ((), (), s32[]{:S(2)}) async-start(), calls=%async_computation.10 | async-start | bytes 2359296 | tf_op jit(solution)/shard_map/reduce_scatter | solution.py:64
  461.0 2.8 copy-start.2
  465.8 109.9 %all-gather.15.cloned.1.call-start = ((), (), s32[]{:S(2)}) async-start(), calls=%async_computation.11 | async-start | bytes 1179648 | tf_op jit(solution)/shard_map/all_gather | solution.py:66
  536.4 116.4 %reduce-scatter.11.cloned.1.call-start = ((), (), s32[]{:S(2)}) async-start(), calls=%async_computation.12 | async-start | bytes 2359296 | tf_op jit(solution)/shard_map/reduce_scatter | solution.py:64
  584.4 68.4 %copy-start.4 = (f32[2,256,128]{1,2,0:T(8,128)S(1)}, f32[2,256,128]{1,2,0:T(8,128)}, u32[]{:S(2)}) copy-start(f32[2,256,128]{1,2,0:T(8,128)} %reduce-scatter.9.cloned.1.call-done) | copy-start | bytes 786436
  584.4 109.3 %all-gather.17.cloned.1.call-start = ((), (), s32[]{:S(2)}) async-start(), calls=%async_computation.13 | async-start | bytes 1179648 | tf_op jit(solution)/shard_map/all_gather | solution.py:66
  654.6 60.9 %all-gather.23.cloned.1.call-start = ((), (), s32[]{:S(2)}) async-start(), calls=%async_computation.17 | async-start | bytes 1310720 | tf_op jit(solution)/shard_map/all_gather | solution.py:34
  693.8 2.7 copy-start.6
  699.6 89.0 %all-reduce.8.cloned.1.call-start = ((), (), s32[]{:S(2)}) async-start(), calls=%async_computation.14 | async-start | bytes 131072 | tf_op jit(solution)/shard_map/psum | solution.py:35
Sparse Core Ops, SparseCore 0:
  13.0 19.4 all-gather.18
  36.4 69.2 all-reduce.3
  124.1 69.1 reduce-scatter.4
  195.7 38.3 all-gather.10
  243.7 67.8 reduce-scatter.6
  314.1 38.4 all-gather.12
  358.6 15.6 all-gather.20
  378.3 69.2 all-reduce.5
  465.9 68.8 reduce-scatter.8
  537.2 38.4 all-gather.14
  584.6 68.2 reduce-scatter.10
  655.3 38.4 all-gather.16
  699.7 15.6 all-gather.22
  719.3 69.2 all-reduce.7
